TPU v7x, 256 devices: a whole 4x4x8 slice. The times are simulated.
256 devices in a mesh: dp: 8 (over x, y_lo), seq: 32 (over z, y_hi, core).
Axes of the slice: x: 4, y: 4 (y_hi: 2, y_lo: 2; y = y_hi * 2 + y_lo), z: 8, core: 2. Of those that a mesh axis runs over, the one named last changes fastest.
Arguments:
- video: bfloat16 [8, 32, 16, 160, 256], P('dp', 'seq'), may hold values from -6 to 6
- cotangent: bfloat16 [8, 32, 16, 160, 256], P('dp', 'seq'), may hold values from -6 to 6
- spatial_weight: bfloat16 [3, 3, 256, 256], replicated, may hold values from -0.125 to 0.125
- temporal_weight: bfloat16 [3, 256, 256], replicated, may hold values from -0.21875 to 0.21875
Outputs:
- video_grad: bfloat16 [8, 32, 16, 160, 256], P('dp', 'seq')
- spatial_grad: float32 [2304, 256], P('seq')
- temporal_grad: float32 [768, 256], P('seq')
All inputs are finite; a program needn't handle non-finite values.
Results may differ from a plain program's by a relative error of at most 0.0054.
Values may be sent and summed in bfloat16 or wider, within the bound.
A program may use at most 128 MiB of HBM per device.

v0:
```python
import jax
import jax.numpy as jnp
from jax import lax
from jax.sharding import PartitionSpec as P


def reduce_grads(partial_sum):
    whole = lax.psum(partial_sum, "dp")
    return lax.psum_scatter(whole, "seq", scatter_dimension=0, tiled=True)


def shards(video, cotangent, spatial_weight, temporal_weight):
    height, width, chans = (video.shape[2], video.shape[3], video.shape[4])
    positions = height * width
    frame = video[0, 0]
    padded = jnp.pad(frame, ((1, 1), (1, 1), (0, 0)))
    hidden = jnp.zeros((height, width, chans), jnp.float32)
    for a in range(3):
        for b in range(3):
            hidden = hidden + jnp.einsum(
                "hwc,cd->hwd",
                padded[a : a + height, b : b + width],
                spatial_weight[a, b],
                preferred_element_type=jnp.float32,
            )
    hidden_low = hidden.astype(jnp.bfloat16)
    grad_flat = cotangent[0, 0].reshape(1, positions, chans)
    hidden_flat = hidden_low.reshape(1, positions, chans)
    total_count = lax.axis_size("dp") * video.shape[0] * lax.axis_size("seq") * positions
    scale = 1.0 / jnp.sqrt(jnp.float32(total_count))
    grad_rows, hidden_rows = (
        lax.all_to_all(grad_flat, "seq", split_axis=1, concat_axis=0, tiled=True),
        lax.all_to_all(hidden_flat, "seq", split_axis=1, concat_axis=0, tiled=True),
    )
    frames = grad_rows.shape[0]
    hid32 = hidden_rows.astype(jnp.float32)
    sig = jax.nn.sigmoid(hid32)
    act = (hid32 * sig).astype(jnp.bfloat16)
    grad_pad = jnp.pad(grad_rows, ((0, 2), (0, 0), (0, 0)))
    act_grad = jnp.zeros(hid32.shape, jnp.float32)
    taps = []
    for k in range(3):
        act_grad = act_grad + jnp.einsum(
            "tqd,cd->tqc",
            grad_pad[k : k + frames],
            temporal_weight[k],
            preferred_element_type=jnp.float32,
        )
        taps.append(
            jnp.einsum(
                "tqc,tqd->cd", act[: frames - k], grad_rows[k:], preferred_element_type=jnp.float32
            )
        )
    temporal_part = jnp.concatenate(taps, axis=0)
    grad_rows_h = (act_grad * sig * (1.0 + hid32 * (1.0 - sig))).astype(jnp.bfloat16)
    back_flat = lax.all_to_all(grad_rows_h, "seq", split_axis=0, concat_axis=1, tiled=True)
    hidden_grad = back_flat.reshape(height, width, chans)
    temporal_grad = reduce_grads(temporal_part) * scale
    grad_pad2 = jnp.pad(hidden_grad, ((1, 1), (1, 1), (0, 0)))
    back = jnp.zeros((height, width, chans), jnp.float32)
    parts = []
    for a in range(3):
        for b in range(3):
            back = back + jnp.einsum(
                "hwd,cd->hwc",
                grad_pad2[2 - a : 2 - a + height, 2 - b : 2 - b + width],
                spatial_weight[a, b],
                preferred_element_type=jnp.float32,
            )
            parts.append(
                jnp.einsum(
                    "hwc,hwd->cd",
                    padded[a : a + height, b : b + width],
                    hidden_grad,
                    preferred_element_type=jnp.float32,
                )
            )
    spatial_grad = reduce_grads(jnp.concatenate(parts, axis=0)) * scale
    video_grad = back.astype(jnp.bfloat16).reshape(video.shape)
    return (video_grad, spatial_grad, temporal_grad)


def solution(mesh):
    placed = (P("dp", "seq", None, None, None), P("dp", "seq", None, None, None), P(), P())
    return jax.shard_map(
        shards,
        mesh=mesh,
        in_specs=placed,
        out_specs=(P("dp", "seq", None, None, None), P("seq", None), P("seq", None)),
        check_vma=False,
    )
```

profile of v0, /device:TPU:2, one launch (start us, length us, event | category | flops | bytes accessed | tf_op | source)
XLA Modules:
  0.0 478.6 jit_solution(2925747647652449)
XLA Ops:
  7.2 4.1 copy.19
  11.8 14.1 %reduce.1 = bf16[2560,256]{1,0:T(8,128)(2,1)} reduce(bf16[2560,1,256]{2,1,0:T(2,128)(2,1)S(1)} %bitcast.204, bf16[]{:T(256)} %broadcast.12), dimensions={1}, to_apply=%bitcast.159.reduce_sub_computation | reduce | bytes 2621442
  25.9 4.1 reshape.59
  30.0 11.9 %all-to-all-start = ((bf16[32,2,10240]{2,1,0:T(2,128)(2,1)}), bf16[32,2,10240]{2,1,0:T(2,128)(2,1)}, u32[]{:S(2)}, u32[]{:S(2)}) async-start(bf16[32,2,10240]{2,1,0:T(2,128)(2,1)} %reshape.59), calls=%async_computation | async-start | bytes 2621440 | tf_op jit(solution)/shard_map/all_to_all | solution.py:32
  46.0 2.2 add_convert_fusion.1
  48.2 16.0 %copy.18 = bf16[1,2560,256]{2,0,1:T(2,128)(2,1)} copy(bf16[1,2560,256]{2,1,0:T(8,128)(2,1)S(1)} %bitcast.206) | data formatting | bytes 2621440 | tf_op jit(solution)/shard_map/reshape | solution.py:28
  64.2 14.1 %reduce = bf16[2560,256]{1,0:T(8,128)(2,1)S(1)} reduce(bf16[2560,1,256]{2,1,0:T(2,128)(2,1)} %bitcast.205, bf16[]{:T(256)} %broadcast.12), dimensions={1}, to_apply=%bitcast.158.reduce_sub_computation | reduce | bytes 2621442
  78.3 1.2 reshape.57
  79.6 9.9 %all-to-all-start.1 = ((bf16[32,2,10240]{2,1,0:T(2,128)(2,1)}), bf16[32,2,10240]{2,1,0:T(2,128)(2,1)}, u32[]{:S(2)}, u32[]{:S(2)}) async-start(bf16[32,2,10240]{2,1,0:T(2,128)(2,1)} %reshape.57), calls=%async_computation.1 | async-start | bytes 2621440 | tf_op jit(solution)/shard_map/all_to_all | solution.py:33
  89.5 8.9 %reshape.60 = bf16[2560,1,256]{2,1,0:T(2,128)(2,1)} reshape(bf16[32,2,10240]{2,1,0:T(2,128)(2,1)} %all-to-all-done) | data formatting | bytes 2621440
  98.3 2.0 copy.12
  100.4 2.0 fusion.93
  102.4 2.0 fusion.95
  104.4 18.8 %all-to-all-done.1 = bf16[32,2,10240]{2,1,0:T(2,128)(2,1)} async-done(((bf16[32,2,10240]{2,1,0:T(2,128)(2,1)}), bf16[32,2,10240]{2,1,0:T(2,128)(2,1)}, u32[]{:S(2)}, u32[]{:S(2)}) %all-to-all-start.1) | async-done | bytes 1310752 | tf_op jit(solution)/shard_map/all_to_all | solution.py:33
  123.2 8.9 %reshape.58 = bf16[2560,1,256]{2,1,0:T(2,128)(2,1)} reshape(bf16[32,2,10240]{2,1,0:T(2,128)(2,1)} %all-to-all-done.1) | data formatting | bytes 2621440
  132.1 2.1 copy.13
  134.2 1.5 copy-done.4
  136.1 2.4 multiply_convert_fusion.1
  138.4 5.6 %all-to-all-start.2 = ((bf16[32,80,256]{2,1,0:T(8,128)(2,1)}), bf16[32,80,256]{2,1,0:T(8,128)(2,1)S(1)}, u32[]{:S(2)}, u32[]{:S(2)}) async-start(bf16[32,80,256]{2,1,0:T(8,128)(2,1)} %multiply_convert_fusion.1), calls=%async_computation.2 | async-start | bytes 2621440 | tf_op jit(solution)/shard_map/all_to_all | solution.py:56
  144.1 4.9 %slice.165 = bf16[1,2480,256]{2,0,1:T(2,128)(2,1)S(1)} slice(bf16[1,2560,256]{2,0,1:T(2,128)(2,1)} %bitcast.195), slice={[0:1], [80:2560], [0:256]} | slice | bytes 2539520 | tf_op jit(solution)/shard_map/slice | solution.py:51
  149.0 2.6 slice.166
  152.1 1.5 copy-done.5
  155.4 0.8 copy-done.3
  156.7 0.9 pad_maximum_fusion
  158.0 20.1 %all-to-all-done.2 = bf16[32,80,256]{2,1,0:T(8,128)(2,1)S(1)} async-done(((bf16[32,80,256]{2,1,0:T(8,128)(2,1)}), bf16[32,80,256]{2,1,0:T(8,128)(2,1)S(1)}, u32[]{:S(2)}, u32[]{:S(2)}) %all-to-all-start.2) | async-done | bytes 1310752 | tf_op jit(solution)/shard_map/all_to_all | solution.py:56
  178.1 1.2 fusion.24
  179.3 1.3 fusion.23
  180.6 1.3 fusion.22
  181.8 1.2 fusion.21
  183.1 1.4 fusion.20
  184.4 1.3 fusion.19
  185.7 1.2 fusion.18
  186.9 1.2 fusion.17
  188.2 1.3 fusion.16
  189.5 84.1 %reduce-scatter.5.cloned.1.call-done = f32[24,256]{1,0:T(8,128)} async-done(((f32[768,256]{1,0:T(8,128)}), f32[24,256]{1,0:T(8,128)}) %reduce-scatter.5.cloned.1.call-update) | async-done | bytes 24592 | tf_op jit(solution)/shard_map/reduce_scatter | solution.py:9
  273.6 31.7 %psum.17 = f32[24,256]{1,0:T(8,128)S(1)} all-reduce(f32[24,256]{1,0:T(8,128)} %reduce-scatter.5.cloned.1.call-done), channel_id=1, replica_groups=mesh['dp'=8,'seq'=32] {'dp'}, use_global_device_ids=true, to_apply=%region_2.3 | all-reduce | flops 6144 | bytes 49152 | tf_op jit(solution)/shard_map/psum | solution.py:8
  305.9 2.0 fusion.10
  307.9 2.0 fusion.12
  309.9 2.0 fusion.14
  311.9 2.0 fusion.2
  314.0 2.0 fusion.4
  316.0 2.0 fusion.6
  318.1 2.1 fusion.8
  320.1 2.1 fusion.82
  322.2 74.5 %reduce-scatter.3.cloned.1.call-done = f32[72,256]{1,0:T(8,128)} async-done(((f32[2304,256]{1,0:T(8,128)}), f32[72,256]{1,0:T(8,128)}) %reduce-scatter.3.cloned.1.call-update) | async-done | bytes 73744 | tf_op jit(solution)/shard_map/reduce_scatter | solution.py:9
  396.7 9.3 %fusion = bf16[1,1,16,160,256]{4,3,2,1,0:T(8,128)(2,1)} fusion(f32[16,160,256]{2,1,0:T(8,128)} %fusion.2, f32[16,160,256]{2,1,0:T(8,128)} %fusion.4, f32[16,160,256]{2,1,0:T(8,128)} %fusion.6, f32[16,160,256]{2,1,0:T(8,128)} %fusion.82, f32[16,160,256]{2,1,0:T(8,128)} %fusion.8, f32[16,160,256]{2,1,0:T(8,128)} %fusion.10, f32[16,160,256]{2,1,0:T(8,128)} %fusion.14, ...), kind=kOutput, calls=%fused_computation.5 | convolution fusion | flops 341442560 | bytes 23724032 | tf_op jit(solution)/shard_map/hwd,cd->hwc/dot_general | solution.py:64
  406.0 64.5 %all-reduce.5.cloned.1.call-done = f32[72,256]{1,0:T(8,128)} async-done(((f32[72,256]{1,0:T(8,128)}), f32[72,256]{1,0:T(8,128)}) %all-reduce.5.cloned.1.call-update) | async-done | bytes 73744 | tf_op jit(solution)/shard_map/psum | solution.py:8
  470.5 1.5 broadcast_multiply_fusion
  (42 shorter events, 8.9 us)
Async XLA Ops:
  30.0 11.9 %copy-start = (bf16[1,1,16,160,256]{4,3,2,1,0:T(8,128)(2,1)S(1)}, bf16[1,1,16,160,256]{4,3,2,1,0:T(8,128)(2,1)}, u32[]{:S(2)}) copy-start(bf16[1,1,16,160,256]{4,3,2,1,0:T(8,128)(2,1)} %param.4) | copy-start | bytes 3932164
  30.0 11.9 %copy-start.6 = (bf16[3,3,256,256]{3,2,1,0:T(8,128)(2,1)S(1)}, bf16[3,3,256,256]{3,2,1,0:T(8,128)(2,1)}, u32[]{:S(2)}) copy-start(bf16[3,3,256,256]{3,2,1,0:T(8,128)(2,1)} %param.6) | copy-start | bytes 3538948
  30.0 49.6 %all-to-all-start = ((bf16[32,2,10240]{2,1,0:T(2,128)(2,1)}), bf16[32,2,10240]{2,1,0:T(2,128)(2,1)}, u32[]{:S(2)}, u32[]{:S(2)}) async-start(bf16[32,2,10240]{2,1,0:T(2,128)(2,1)} %reshape.59), calls=%async_computation | async-start | bytes 2621440 | tf_op jit(solution)/shard_map/all_to_all | solution.py:32
  79.6 43.6 %all-to-all-start.1 = ((bf16[32,2,10240]{2,1,0:T(2,128)(2,1)}), bf16[32,2,10240]{2,1,0:T(2,128)(2,1)}, u32[]{:S(2)}, u32[]{:S(2)}) async-start(bf16[32,2,10240]{2,1,0:T(2,128)(2,1)} %reshape.57), calls=%async_computation.1 | async-start | bytes 2621440 | tf_op jit(solution)/shard_map/all_to_all | solution.py:33
  98.3 2.0 copy-start.10
  100.4 33.8 %copy-start.2 = (bf16[1,2560,256]{2,1,0:T(8,128)(2,1)}, bf16[1,2560,256]{2,1,0:T(8,128)(2,1)S(1)}, u32[]{:S(2)}) copy-start(bf16[1,2560,256]{2,1,0:T(8,128)(2,1)S(1)} %copy.12) | copy-start | bytes 3932164
  132.1 3.6 copy-start.8
  132.1 4.0 copy-start.9
  134.2 1.6 copy-start.4
  138.4 39.6 %all-to-all-start.2 = ((bf16[32,80,256]{2,1,0:T(8,128)(2,1)}), bf16[32,80,256]{2,1,0:T(8,128)(2,1)S(1)}, u32[]{:S(2)}, u32[]{:S(2)}) async-start(bf16[32,80,256]{2,1,0:T(8,128)(2,1)} %multiply_convert_fusion.1), calls=%async_computation.2 | async-start | bytes 2621440 | tf_op jit(solution)/shard_map/all_to_all | solution.py:56
  144.0 129.5 %reduce-scatter.5.cloned.1.call-start = ((), (), s32[]{:S(2)}) async-start(), calls=%async_computation.7 | async-start | bytes 811008 | tf_op jit(solution)/shard_map/reduce_scatter | solution.py:9
  144.1 4.9 %copy-start.1 = (bf16[2560,1,256]{2,1,0:T(2,128)(2,1)S(1)}, bf16[2560,1,256]{2,1,0:T(2,128)(2,1)}, u32[]{:S(2)}) copy-start(bf16[2560,1,256]{2,1,0:T(2,128)(2,1)} %reshape.60) | copy-start | bytes 3932164
  151.8 1.7 copy-start.5
  154.9 1.3 copy-start.3
  157.7 239.0 %reduce-scatter.3.cloned.1.call-start = ((), (), s32[]{:S(2)}) async-start(), calls=%async_computation.5 | async-start | bytes 2433024 | tf_op jit(solution)/shard_map/reduce_scatter | solution.py:9
  189.4 116.5 %copy-start.7 = (bf16[3,3,256,256]{3,2,1,0:T(8,128)(2,1)S(1)}, bf16[3,3,256,256]{3,2,1,0:T(8,128)(2,1)}, u32[]{:S(2)}) copy-start(bf16[3,3,256,256]{3,2,1,0:T(8,128)(2,1)} %param.6) | copy-start | bytes 3538948
  189.4 281.1 %all-reduce.5.cloned.1.call-start = ((), (), s32[]{:S(2)}) async-start(), calls=%async_computation.6 | async-start | bytes 147456 | tf_op jit(solution)/shard_map/psum | solution.py:8
Sparse Core Ops, SparseCore 0:
  157.8 115.7 reduce-scatter.4
  278.3 118.3 reduce-scatter.2
  399.3 71.1 all-reduce.4
where the time goes:
time: 480 us; the launch traced here: 479 us
  waiting for transfers between devices  262 us (55%)
  local copies, waits for them, and re-layouts  59.8 us (12%)
  matrix products  51.3 us (11%)
  other arithmetic  32.1 us (7%)
  blocking collectives  31.7 us (7%)
  starting transfers between devices  27.8 us (6%)
  between operations  14 us (3%)
    reduce_scatter x2, waiting for transfers between devices, reduce_grads(): return lax.psum_scatter(whole, 'seq', scatter_dimension=0, tiled=True)  159 us
    psum x1, waiting for transfers between devices, reduce_grads(): whole = lax.psum(partial_sum, 'dp')  64.5 us
    unnamed x31, local copies, waits for them, and re-layouts  32.3 us
    psum x1, blocking collectives, reduce_grads(): whole = lax.psum(partial_sum, 'dp')  31.7 us
    unnamed x2, other arithmetic  28.3 us
    dot_general x9, matrix products, shards(): jnp.einsum('hwd,cd->hwc', grad_pad2[2 - a:2 - a + height, 2 - b:2 - b + w...  25.6 us
    all_to_all x1, waiting for transfers between devices, shards(): lax.all_to_all(grad_rows_h, 'seq', split_axis=0, concat_axis=1, tiled=True)  20.1 us
    all_to_all x1, waiting for transfers between devices, shards(): lax.all_to_all(hidden_flat, 'seq', split_axis=1, concat_axis=0, tiled=True)  18.8 us
  transfers between devices with their start and end apart: 6, of which 5 were waited for; matrix products, arithmetic and copies ran while one was open for 21% of the time, Pallas kernels for 0%

commit v1 on v0

--- a/solution.py
+++ b/solution.py
@@ -5,7 +5,8 @@
 
 
 def reduce_grads(partial_sum):
-    whole = lax.psum(partial_sum, "dp")
+    pieces = lax.all_gather(partial_sum, "dp")
+    whole = jnp.sum(pieces, axis=0)
     return lax.psum_scatter(whole, "seq", scatter_dimension=0, tiled=True)
 
 

time: 480 us -> 904 us (1.88)
  waiting for transfers between devices: 262 us -> 692 us
  matrix products: 51.3 us -> 27.4 us
  other arithmetic: 32.1 us -> 46.2 us
  blocking collectives: 31.7 us -> 41.3 us
    all_gather x0 -> x2, waiting for transfers between devices: none -> 453 us  [reduce_grads(): pieces = lax.all_gather(partial_sum, 'dp')]
    reduce_scatter x2, waiting for transfers between devices: 159 us -> 224 us  [reduce_grads(): return lax.psum_scatter(whole, 'seq', scatter_dimension=0, tiled=True)]
    psum x1 -> x0, waiting for transfers between devices: 64.5 us -> none  [reduce_grads(): whole = lax.psum(partial_sum, 'dp')]
    all_to_all x0 -> x1, blocking collectives: none -> 41.3 us  [shards(): lax.all_to_all(grad_rows_h, 'seq', split_axis=0, concat_axis=1, tiled=True)]
    psum x1 -> x0, blocking collectives: 31.7 us -> none  [reduce_grads(): whole = lax.psum(partial_sum, 'dp')]
    all_to_all x1 -> x0, waiting for transfers between devices: 20.1 us -> none  [shards(): lax.all_to_all(grad_rows_h, 'seq', split_axis=0, concat_axis=1, tiled=True)]
    dot_general x9, matrix products: 25.6 us -> 6.7 us  [shards(): jnp.einsum('hwd,cd->hwc', grad_pad2[2 - a:2 - a + height, 2 - b:2 - b + w...]
    reduce_sum x0 -> x2, other arithmetic: none -> 13.5 us  [reduce_grads(): whole = jnp.sum(pieces, axis=0)]
  transfers between devices with their start and end apart: 6 -> 6, of which waited for: 5 -> 5; matrix products, arithmetic and copies ran while one was open for 21% -> 10% of each run, Pallas kernels for 0% -> 0%
where the time goes in v1:
time: 904 us; the launch traced here: 903 us
  waiting for transfers between devices  692 us (77%)
  local copies, waits for them, and re-layouts  60.4 us (7%)
  other arithmetic  46.2 us (5%)
  blocking collectives  41.3 us (5%)
  matrix products  27.4 us (3%)
  starting transfers between devices  21.9 us (2%)
  between operations  13.9 us (2%)
    all_gather x2, waiting for transfers between devices, reduce_grads(): pieces = lax.all_gather(partial_sum, 'dp')  453 us
    reduce_scatter x2, waiting for transfers between devices, reduce_grads(): return lax.psum_scatter(whole, 'seq', scatter_dimension=0, tiled=True)  224 us
    all_to_all x1, blocking collectives, shards(): lax.all_to_all(grad_rows_h, 'seq', split_axis=0, concat_axis=1, tiled=True)  41.3 us
    unnamed x27, local copies, waits for them, and re-layouts  29.3 us
    unnamed x2, other arithmetic  28.2 us
  transfers between devices with their start and end apart: 6, of which 5 were waited for; matrix products, arithmetic and copies ran while one was open for 10% of the time, Pallas kernels for 0%

profile of v1, /device:TPU:2, one launch (start us, length us, event | category | flops | bytes accessed | tf_op | source)
XLA Modules:
  0.0 902.8 jit_solution(14301364525738051040)
XLA Ops:
  7.2 5.2 copy.19
  12.9 14.1 %reduce.1 = bf16[2560,256]{1,0:T(8,128)(2,1)S(1)} reduce(bf16[2560,1,256]{2,1,0:T(2,128)(2,1)} %bitcast.207, bf16[]{:T(256)} %broadcast.12), dimensions={1}, to_apply=%bitcast.161.reduce_sub_computation | reduce | bytes 2621442
  27.0 1.2 reshape.61
  28.3 11.9 %all-to-all-start = ((bf16[32,2,10240]{2,1,0:T(2,128)(2,1)}), bf16[32,2,10240]{2,1,0:T(2,128)(2,1)}, u32[]{:S(2)}, u32[]{:S(2)}) async-start(bf16[32,2,10240]{2,1,0:T(2,128)(2,1)} %reshape.61), calls=%async_computation | async-start | bytes 2621440 | tf_op jit(solution)/shard_map/all_to_all | solution.py:33
  44.3 1.3 add_convert_fusion.1
  45.6 16.0 %copy.18 = bf16[1,2560,256]{2,0,1:T(2,128)(2,1)} copy(bf16[1,2560,256]{2,1,0:T(8,128)(2,1)S(1)} %bitcast.210) | data formatting | bytes 2621440 | tf_op jit(solution)/shard_map/reshape | solution.py:29
  61.6 14.1 %reduce = bf16[2560,256]{1,0:T(8,128)(2,1)S(1)} reduce(bf16[2560,1,256]{2,1,0:T(2,128)(2,1)} %bitcast.208, bf16[]{:T(256)} %broadcast.12), dimensions={1}, to_apply=%bitcast.160.reduce_sub_computation | reduce | bytes 2621442
  75.7 1.2 reshape.59
  76.9 9.6 %all-to-all-start.1 = ((bf16[32,2,10240]{2,1,0:T(2,128)(2,1)}), bf16[32,2,10240]{2,1,0:T(2,128)(2,1)}, u32[]{:S(2)}, u32[]{:S(2)}) async-start(bf16[32,2,10240]{2,1,0:T(2,128)(2,1)} %reshape.59), calls=%async_computation.1 | async-start | bytes 2621440 | tf_op jit(solution)/shard_map/all_to_all | solution.py:34
  86.8 8.9 reshape.62
  95.7 6.1 slice.165
  101.8 3.9 slice.166
  105.9 14.7 %all-to-all-done.1 = bf16[32,2,10240]{2,1,0:T(2,128)(2,1)} async-done(((bf16[32,2,10240]{2,1,0:T(2,128)(2,1)}), bf16[32,2,10240]{2,1,0:T(2,128)(2,1)}, u32[]{:S(2)}, u32[]{:S(2)}) %all-to-all-start.1) | async-done | bytes 1310752 | tf_op jit(solution)/shard_map/all_to_all | solution.py:34
  120.6 8.9 reshape.60
  129.5 1.9 copy.13
  131.4 0.7 multiply_convert_fusion
  132.1 0.8 copy-done.2
  132.9 1.2 copy-done.4
  134.3 1.5 copy-done.5
  137.1 0.5 convolution_bitcast_fusion.2
  137.7 0.9 pad_maximum_fusion
  139.8 1.2 copy-done.3
  141.0 1.3 multiply_convert_fusion.1
  142.3 41.3 %all_to_all.30 = bf16[32,80,256]{2,1,0:T(8,128)(2,1)S(1)} all-to-all(bf16[32,80,256]{2,1,0:T(8,128)(2,1)S(1)} %multiply_convert_fusion.1), channel_id=1, replica_groups=mesh['dp'=8,'seq'=32] {'seq'}, dimensions={0} | all-to-all | bytes 2621440 | tf_op jit(solution)/shard_map/all_to_all | solution.py:57
  183.6 1.3 fusion.24
  184.9 1.2 fusion.23
  186.2 1.3 fusion.22
  187.4 1.3 fusion.21
  188.7 1.3 fusion.20
  190.0 1.2 fusion.19
  191.2 1.2 fusion.18
  192.5 1.2 fusion.17
  193.7 1.3 fusion.16
  195.1 86.8 %all-gather.7.cloned.1.call-done = f32[6144,256]{1,0:T(8,128)} async-done(((f32[768,256]{1,0:T(8,128)}), f32[6144,256]{1,0:T(8,128)}) %all-gather.7.cloned.1.call-update) | async-done | bytes 6291472 | tf_op jit(solution)/shard_map/all_gather | solution.py:8
  281.9 4.2 reduce_sum.19
  286.1 366.1 %all-gather.5.cloned.1.call-done = f32[18432,256]{1,0:T(8,128)} async-done(((f32[2304,256]{1,0:T(8,128)}), f32[18432,256]{1,0:T(8,128)}) %all-gather.5.cloned.1.call-update) | async-done | bytes 18874384 | tf_op jit(solution)/shard_map/all_gather | solution.py:8
  652.2 9.3 %reduce_sum.18 = f32[2304,256]{1,0:T(8,128)} reduce(f32[8,2304,256]{2,1,0:T(8,128)} %bitcast.203, f32[]{:T(128)} %constant.2.clone.1), dimensions={0}, to_apply=%region_0.1 | reduce | flops 4128768 | bytes 21233668 | tf_op jit(solution)/shard_map/reduce_sum | solution.py:9
  661.5 1.2 copy-done.7
  662.8 0.5 fusion.10
  663.9 0.6 fusion.14
  664.9 0.5 fusion.4
  665.5 0.6 fusion.6
  666.0 0.6 fusion.8
  667.1 2.4 fusion
  669.5 102.3 %reduce-scatter.5.cloned.1.call-done = f32[24,256]{1,0:T(8,128)} async-done(((f32[768,256]{1,0:T(8,128)}), f32[24,256]{1,0:T(8,128)}) %reduce-scatter.5.cloned.1.call-update) | async-done | bytes 24592 | tf_op jit(solution)/shard_map/reduce_scatter | solution.py:10
  771.8 1.3 broadcast_multiply_fusion.1
  773.1 121.6 %reduce-scatter.3.cloned.1.call-done = f32[72,256]{1,0:T(8,128)} async-done(((f32[2304,256]{1,0:T(8,128)}), f32[72,256]{1,0:T(8,128)}) %reduce-scatter.3.cloned.1.call-update) | async-done | bytes 73744 | tf_op jit(solution)/shard_map/reduce_scatter | solution.py:10
  894.8 1.5 broadcast_multiply_fusion
  (41 shorter events, 9.7 us)
Async XLA Ops:
  28.3 11.9 %copy-start = (bf16[1,1,16,160,256]{4,3,2,1,0:T(8,128)(2,1)S(1)}, bf16[1,1,16,160,256]{4,3,2,1,0:T(8,128)(2,1)}, u32[]{:S(2)}) copy-start(bf16[1,1,16,160,256]{4,3,2,1,0:T(8,128)(2,1)} %param.4) | copy-start | bytes 3932164
  28.3 11.9 %copy-start.6 = (bf16[3,3,256,256]{3,2,1,0:T(8,128)(2,1)S(1)}, bf16[3,3,256,256]{3,2,1,0:T(8,128)(2,1)}, u32[]{:S(2)}) copy-start(bf16[3,3,256,256]{3,2,1,0:T(8,128)(2,1)} %param.6) | copy-start | bytes 3538948
  28.3 48.7 %all-to-all-start = ((bf16[32,2,10240]{2,1,0:T(2,128)(2,1)}), bf16[32,2,10240]{2,1,0:T(2,128)(2,1)}, u32[]{:S(2)}, u32[]{:S(2)}) async-start(bf16[32,2,10240]{2,1,0:T(2,128)(2,1)} %reshape.61), calls=%async_computation | async-start | bytes 2621440 | tf_op jit(solution)/shard_map/all_to_all | solution.py:33
  76.9 43.7 %all-to-all-start.1 = ((bf16[32,2,10240]{2,1,0:T(2,128)(2,1)}), bf16[32,2,10240]{2,1,0:T(2,128)(2,1)}, u32[]{:S(2)}, u32[]{:S(2)}) async-start(bf16[32,2,10240]{2,1,0:T(2,128)(2,1)} %reshape.59), calls=%async_computation.1 | async-start | bytes 2621440 | tf_op jit(solution)/shard_map/all_to_all | solution.py:34
  86.6 195.3 %all-gather.7.cloned.1.call-start = ((), (), s32[]{:S(2)}) async-start(), calls=%async_computation.8 | async-start | bytes 7077888 | tf_op jit(solution)/shard_map/all_gather | solution.py:8
  95.7 6.1 copy-start.1
  131.4 1.5 copy-start.2
  131.4 2.7 copy-start.4
  134.1 1.7 copy-start.5
  137.7 1.1 copy-start.8
  138.6 513.6 %all-gather.5.cloned.1.call-start = ((), (), s32[]{:S(2)}) async-start(), calls=%async_computation.7 | async-start | bytes 21233664 | tf_op jit(solution)/shard_map/all_gather | solution.py:8
  139.3 1.7 copy-start.3
  195.0 576.8 %reduce-scatter.5.cloned.1.call-start = ((), (), s32[]{:S(2)}) async-start(), calls=%async_computation.6 | async-start | bytes 811008 | tf_op jit(solution)/shard_map/reduce_scatter | solution.py:10
  286.1 608.7 %reduce-scatter.3.cloned.1.call-start = ((), (), s32[]{:S(2)}) async-start(), calls=%async_computation.5 | async-start | bytes 2433024 | tf_op jit(solution)/shard_map/reduce_scatter | solution.py:10
  661.5 1.3 copy-start.7
Sparse Core Ops, SparseCore 0:
  138.7 143.0 all-gather.6
  283.7 368.5 all-gather.4
  656.2 115.4 reduce-scatter.4
  776.4 118.3 reduce-scatter.2
